TPU v7x, 128 devices: a whole 4x4x4 slice. The times are simulated.
128 devices in a mesh: rollout: 4 (over y_lo, core), row: 8 (over x, y_hi), col: 4 (over z).
Axes of the slice: x: 4, y: 4 (y_hi: 2, y_lo: 2; y = y_hi * 2 + y_lo), z: 4, core: 2. Of those that a mesh axis runs over, the one named last changes fastest.
Arguments:
- queries: bfloat16 [16384, 4096], P(('rollout', 'row', 'col')), may hold values from -16 to 16
- keys: bfloat16 [16384, 512], P(('rollout', 'row', 'col')), may hold values from -16 to 16
- values: bfloat16 [16384, 512], P(('rollout', 'row', 'col')), may hold values from -6 to 6
- out_grad: bfloat16 [16384, 4096], P(('rollout', 'row', 'col')), may hold values from -12 to 12
- hidden_in: bfloat16 [16384, 8192], P(('rollout', 'col'), 'row'), may hold values from -1.5 to 1.5
- q_weight: bfloat16 [4096, 8192], P('col', 'row'), may hold values from -0.09375 to 0.09375
- lengths: int32 [4, 32], P('rollout'), may hold values from 1 to 256, 4096 in all within a row
- kv_order: int32 [4], replicated, may hold values from 0 to 3, each once
Outputs:
- key_grad: float32 [16384, 512], P(('rollout', 'row', 'col'))
- value_grad: float32 [16384, 512], P(('rollout', 'row', 'col'))
- input_grad: bfloat16 [16384, 8192], P(('rollout', 'col'), 'row')
- weight_grad: float32 [4096, 8192], P(('rollout', 'col'), 'row')
Inputs may be any that keep to these rules, and one draw needn't show every extreme that they name: `lengths`: each row lists, for 16 packed rollouts in order, a prompt length and then a response length; a row sums to 4096 and its largest entry is exactly 256. `kv_order`: A permutation of the 4 key-value heads.
All inputs are finite; a program needn't handle non-finite values.
Results may differ from a plain program's by a relative error of at most 0.0057.
Values may be sent and summed in bfloat16 or wider, within the bound.
No kernel may reach another device: no remote copies, remote signals or barrier semaphores. Data moves between devices by JAX's collectives and lax.ppermute only.
A program may use at most 192 MiB of HBM per device.

v0:
```python
import math
import jax
import jax.numpy as jnp
from jax import lax
from jax.sharding import PartitionSpec as P

HQ = 32
KV = 4
HD = 128
ROLLS = 16


def token_parts(lengths_row, length_total):
    bounds = jnp.cumsum(lengths_row)
    position = jnp.arange(length_total, dtype=jnp.int32)
    return jnp.sum((position[:, None] >= bounds[None, :]).astype(jnp.int32), axis=1)


def attend_head(query_all, key_all, value_all, grad_all, document, row_block, reach):
    length_total = query_all.shape[0]
    scale_factor = 1.0 / math.sqrt(query_all.shape[1])
    position = jnp.arange(length_total, dtype=jnp.int32)
    grad_key = jnp.zeros(key_all.shape, jnp.float32)
    grad_value = jnp.zeros(value_all.shape, jnp.float32)
    query_pieces = []
    for row_begin in range(0, length_total, row_block):
        row_end = row_begin + row_block
        key_first = max(0, row_begin - reach)
        query_rows = query_all[row_begin:row_end]
        grad_rows = grad_all[row_begin:row_end]
        key_rows = key_all[key_first:row_end]
        value_rows = value_all[key_first:row_end]
        allowed = (position[None, key_first:row_end] <= position[row_begin:row_end, None]) & (
            document[None, key_first:row_end] == document[row_begin:row_end, None]
        )
        raw_scores = (
            jnp.einsum("qd,kd->qk", query_rows, key_rows, preferred_element_type=jnp.float32)
            * scale_factor
        )
        raw_scores = jnp.where(allowed, raw_scores, -jnp.inf)
        row_top = jnp.max(raw_scores, axis=1, keepdims=True)
        exp_scores = jnp.exp(raw_scores - row_top)
        attention = exp_scores / jnp.sum(exp_scores, axis=1, keepdims=True)
        attention_half = attention.astype(jnp.bfloat16)
        grad_value = grad_value.at[key_first:row_end].add(
            jnp.einsum("qk,qd->kd", attention_half, grad_rows, preferred_element_type=jnp.float32)
        )
        grad_attention = jnp.einsum(
            "qd,kd->qk", grad_rows, value_rows, preferred_element_type=jnp.float32
        )
        row_delta = jnp.sum(attention * grad_attention, axis=1, keepdims=True)
        grad_scores = (attention * (grad_attention - row_delta) * scale_factor).astype(jnp.bfloat16)
        query_pieces.append(
            jnp.dot(grad_scores, key_rows, preferred_element_type=jnp.float32).astype(jnp.bfloat16)
        )
        grad_key = grad_key.at[key_first:row_end].add(
            jnp.einsum("qk,qd->kd", grad_scores, query_rows, preferred_element_type=jnp.float32)
        )
    return (jnp.concatenate(query_pieces, axis=0), grad_key, grad_value)


def body(queries, keys, values, out_grad, hidden_in, q_weight, lengths, kv_order):
    group_size = lax.axis_size(("row", "col"))
    rows_count = lax.axis_size("row")
    columns_count = lax.axis_size("col")
    token_dev = queries.shape[0]
    length_total = token_dev * group_size
    heads_dev = HQ // group_size
    sources_each = HQ // KV // heads_dev
    reach = 2 * (length_total // ROLLS)
    head_query, head_grad = (
        lax.all_to_all(queries, ("row", "col"), split_axis=1, concat_axis=0, tiled=True),
        lax.all_to_all(out_grad, ("row", "col"), split_axis=1, concat_axis=0, tiled=True),
    )
    kv_range = jnp.arange(KV, dtype=jnp.int32)
    owner = jnp.arange(group_size, dtype=jnp.int32) // sources_each
    chosen = jnp.sum(jnp.where(owner[:, None] == kv_range[None, :], kv_order[None, :], 0), axis=1)
    pick_table = (kv_range[:, None] == chosen[None, :]).astype(jnp.bfloat16)
    key_send = jnp.einsum(
        "tkd,kj->tjd",
        keys.reshape(token_dev, KV, HD),
        pick_table,
        preferred_element_type=jnp.float32,
    ).astype(jnp.bfloat16)
    value_send = jnp.einsum(
        "tkd,kj->tjd",
        values.reshape(token_dev, KV, HD),
        pick_table,
        preferred_element_type=jnp.float32,
    ).astype(jnp.bfloat16)
    key_got, value_got = (
        lax.all_to_all(key_send, ("row", "col"), split_axis=1, concat_axis=0, tiled=True),
        lax.all_to_all(value_send, ("row", "col"), split_axis=1, concat_axis=0, tiled=True),
    )
    key_full = key_got.reshape(length_total, HD)
    value_full = value_got.reshape(length_total, HD)
    parts = token_parts(lengths[0], length_total)
    document = parts // 2
    response = (parts % 2).astype(jnp.bfloat16)
    head_grad = head_grad * response[:, None]
    row_block = min(512, length_total)
    grad_query, grad_key, grad_value = attend_head(
        head_query, key_full, value_full, head_grad, document, row_block, reach
    )
    key_back, value_back = (
        lax.all_to_all(
            grad_key.reshape(group_size, token_dev, HD),
            ("row", "col"),
            split_axis=0,
            concat_axis=0,
            tiled=True,
        ),
        lax.all_to_all(
            grad_value.reshape(group_size, token_dev, HD),
            ("row", "col"),
            split_axis=0,
            concat_axis=0,
            tiled=True,
        ),
    )
    order_table = (kv_order[:, None] == kv_range[None, :]).astype(jnp.float32)

    def place_heads(stacked):
        summed = jnp.sum(stacked.reshape(KV, sources_each, token_dev, HD), axis=1)
        placed = jnp.einsum("mtd,mk->tkd", summed, order_table, precision=lax.Precision.HIGHEST)
        return placed.reshape(token_dev, KV * HD)

    key_grad = place_heads(key_back)
    value_grad = place_heads(value_back)
    arranged = grad_query.reshape(columns_count, rows_count, token_dev, heads_dev * HD)
    arranged = arranged.transpose(1, 0, 2, 3).reshape(length_total, heads_dev * HD)
    shard_query = lax.all_to_all(arranged, ("row", "col"), split_axis=0, concat_axis=1, tiled=True)
    block_query = lax.all_gather(shard_query, "row", axis=0, tiled=True)
    used = block_query
    input_grad = jnp.dot(
        used,
        lax.all_gather(q_weight, "col", axis=0, tiled=True),
        preferred_element_type=jnp.float32,
    ).astype(jnp.bfloat16)
    used = block_query
    weight_grad = lax.psum_scatter(
        lax.dot_general(
            used, hidden_in, (((0,), (0,)), ((), ())), preferred_element_type=jnp.float32
        ),
        ("rollout", "col"),
        scatter_dimension=0,
        tiled=True,
    )
    return (key_grad, value_grad, input_grad, weight_grad)


def solution(mesh):
    placed = (
        P(("rollout", "row", "col"), None),
        P(("rollout", "row", "col"), None),
        P(("rollout", "row", "col"), None),
        P(("rollout", "row", "col"), None),
        P(("rollout", "col"), "row"),
        P("col", "row"),
        P("rollout", None),
        P(),
    )
    return jax.shard_map(
        body,
        mesh=mesh,
        in_specs=placed,
        out_specs=(
            P(("rollout", "row", "col"), None),
            P(("rollout", "row", "col"), None),
            P(("rollout", "col"), "row"),
            P(("rollout", "col"), "row"),
        ),
        check_vma=False,
    )
```

profile of v0, /device:TPU:1, one launch (start us, length us, event | category | flops | bytes accessed | tf_op | source)
XLA Modules:
  0.0 613.1 jit_solution(12362430108168158145)
XLA Ops:
  10.9 11.5 %all-to-all-start = ((bf16[128,32,128]{2,0,1:T(8,128)(2,1)}), bf16[128,32,128]{2,0,1:T(8,128)(2,1)S(1)}, u32[]{:S(2)}, u32[]{:S(2)}) async-start(bf16[128,32,128]{2,0,1:T(8,128)(2,1)} %copy.141), calls=%async_computation | async-start | bytes 2097152 | tf_op jit(solution)/shard_map/all_to_all | solution.py:92
  24.7 13.9 %all-to-all-done = bf16[128,32,128]{2,0,1:T(8,128)(2,1)S(1)} async-done(((bf16[128,32,128]{2,0,1:T(8,128)(2,1)}), bf16[128,32,128]{2,0,1:T(8,128)(2,1)S(1)}, u32[]{:S(2)}, u32[]{:S(2)}) %all-to-all-start) | async-done | bytes 1048608 | tf_op jit(solution)/shard_map/all_to_all | solution.py:92
  38.6 6.0 all-to-all-start.1
  46.4 2.6 copy.147
  56.5 3.5 all-to-all-done.1
  60.0 6.9 %all-to-all-start.3 = ((bf16[128,32,128]{2,0,1:T(8,128)(2,1)}), bf16[128,32,128]{2,0,1:T(8,128)(2,1)}, u32[]{:S(2)}, u32[]{:S(2)}) async-start(bf16[128,32,128]{2,0,1:T(8,128)(2,1)} %copy.147), calls=%async_computation.3 | async-start | bytes 2097152 | tf_op jit(solution)/shard_map/all_to_all | solution.py:93
  70.1 12.2 %all-to-all-done.3 = bf16[128,32,128]{2,0,1:T(8,128)(2,1)} async-done(((bf16[128,32,128]{2,0,1:T(8,128)(2,1)}), bf16[128,32,128]{2,0,1:T(8,128)(2,1)}, u32[]{:S(2)}, u32[]{:S(2)}) %all-to-all-start.3) | async-done | bytes 1048608 | tf_op jit(solution)/shard_map/all_to_all | solution.py:93
  82.3 6.9 %all-to-all-start.2 = ((bf16[128,32,128]{0,2,1:T(8,128)(2,1)}), bf16[128,32,128]{0,2,1:T(8,128)(2,1)}, u32[]{:S(2)}, u32[]{:S(2)}) async-start(bf16[128,32,128]{0,2,1:T(8,128)(2,1)} %bitcast.153), calls=%async_computation.2 | async-start | bytes 2097152 | tf_op jit(solution)/shard_map/all_to_all | solution.py:73
  95.7 2.8 fusion.102
  98.5 6.0 all-to-all-done.2
  146.6 22.1 %all_to_all.94 = bf16[32,128,128]{2,1,0:T(8,128)(2,1)} all-to-all(bf16[32,128,128]{2,1,0:T(8,128)(2,1)S(1)} %bitcast.156), channel_id=1, replica_groups=mesh['rollout'=4,'row'=8,'col'=4] {'row','col'}, dimensions={0} | all-to-all | bytes 2097152 | tf_op jit(solution)/shard_map/all_to_all | solution.py:132
  171.7 118.2 %all-gather.3.cloned.1.call-done = bf16[1024,4096]{0,1:T(8,128)(2,1)} async-done(((bf16[128,4096]{0,1:T(8,128)(2,1)}), bf16[1024,4096]{0,1:T(8,128)(2,1)}) %all-gather.3.cloned.1.call-update) | async-done | bytes 8388624 | tf_op jit(solution)/shard_map/all_gather | solution.py:133
  289.9 15.2 %fusion.114 = f32[4096,1024]{1,0:T(8,128)} fusion(bf16[1024,4096]{0,1:T(8,128)(2,1)} %all-gather.3.cloned.1.call-done, bf16[1024,1024]{1,0:T(8,128)(2,1)S(1)} %copy-done), kind=kOutput, calls=%fused_computation.197 | convolution fusion | flops 8589934592 | bytes 27262976 | tf_op jit(solution)/shard_map/dot_general | solution.py:142
  323.4 6.6 %all-to-all-start.4 = ((f32[32,128,128]{2,1,0:T(8,128)}), f32[32,128,128]{2,1,0:T(8,128)S(1)}, u32[]{:S(2)}, u32[]{:S(2)}) async-start(f32[32,128,128]{2,1,0:T(8,128)} %bitcast.48), calls=%async_computation.4 | async-start | bytes 4194304 | tf_op jit(solution)/shard_map/all_to_all | solution.py:106
  335.5 2.5 fusion.23
  338.0 2.5 fusion.22
  340.6 2.5 fusion.21
  343.1 2.5 fusion.20
  350.4 6.6 %all-to-all-done.4 = f32[32,128,128]{2,1,0:T(8,128)S(1)} async-done(((f32[32,128,128]{2,1,0:T(8,128)}), f32[32,128,128]{2,1,0:T(8,128)S(1)}, u32[]{:S(2)}, u32[]{:S(2)}) %all-to-all-start.4) | async-done | bytes 2097184 | tf_op jit(solution)/shard_map/all_to_all | solution.py:106
  357.0 10.1 %all-to-all-start.5 = ((f32[32,128,128]{2,1,0:T(8,128)}), f32[32,128,128]{2,1,0:T(8,128)}, u32[]{:S(2)}, u32[]{:S(2)}) async-start(f32[32,128,128]{2,1,0:T(8,128)} %bitcast.51), calls=%async_computation.5 | async-start | bytes 4194304 | tf_op jit(solution)/shard_map/all_to_all | solution.py:113
  369.0 26.8 %all-to-all-done.5 = f32[32,128,128]{2,1,0:T(8,128)} async-done(((f32[32,128,128]{2,1,0:T(8,128)}), f32[32,128,128]{2,1,0:T(8,128)}, u32[]{:S(2)}, u32[]{:S(2)}) %all-to-all-start.5) | async-done | bytes 2097184 | tf_op jit(solution)/shard_map/all_to_all | solution.py:113
  398.8 21.5 %all-gather.5.cloned.1.call-done = bf16[4096,1024]{1,0:T(8,128)(2,1)} async-done(((bf16[1024,1024]{1,0:T(8,128)(2,1)}), bf16[4096,1024]{1,0:T(8,128)(2,1)}) %all-gather.5.cloned.1.call-update) | async-done | bytes 8388624 | tf_op jit(solution)/shard_map/all_gather | solution.py:137
  420.3 14.8 %convolution_convert_fusion = bf16[1024,1024]{1,0:T(8,128)(2,1)} fusion(bf16[1024,4096]{0,1:T(8,128)(2,1)} %all-gather.3.cloned.1.call-done, bf16[4096,1024]{1,0:T(8,128)(2,1)} %all-gather.5.cloned.1.call-done), kind=kOutput, calls=%fused_computation.30 | convolution fusion | flops 8590983168 | bytes 18874368 | tf_op jit(solution)/shard_map/dot_general | solution.py:135
  435.1 171.2 %reduce-scatter.2.cloned.1.call-done = f32[256,1024]{1,0:T(8,128)} async-done(((f32[4096,1024]{1,0:T(8,128)}), f32[256,1024]{1,0:T(8,128)}) %reduce-scatter.2.cloned.1.call-update) | async-done | bytes 1048592 | tf_op jit(solution)/shard_map/reduce_scatter | solution.py:141
  (347 shorter events, 102.5 us)
Async XLA Ops:
  7.2 282.7 %copy-start = (bf16[1024,1024]{1,0:T(8,128)(2,1)S(1)}, bf16[1024,1024]{1,0:T(8,128)(2,1)}, u32[]{:S(2)}) copy-start(bf16[1024,1024]{1,0:T(8,128)(2,1)} %param.44) | copy-start | bytes 6291460
  10.9 13.8 %copy-start.62 = (bf16[128,512]{1,0:T(8,128)(2,1)S(1)}, bf16[128,512]{1,0:T(8,128)(2,1)}, u32[]{:S(2)}) copy-start(bf16[128,512]{1,0:T(8,128)(2,1)} %param.42) | copy-start | bytes 393220
  10.9 27.7 %all-to-all-start = ((bf16[128,32,128]{2,0,1:T(8,128)(2,1)}), bf16[128,32,128]{2,0,1:T(8,128)(2,1)S(1)}, u32[]{:S(2)}, u32[]{:S(2)}) async-start(bf16[128,32,128]{2,0,1:T(8,128)(2,1)} %copy.141), calls=%async_computation | async-start | bytes 2097152 | tf_op jit(solution)/shard_map/all_to_all | solution.py:92
  24.7 21.5 %copy-start.117 = (s32[1,32]{1,0:T(1,128)S(1)}, s32[1,32]{1,0:T(1,128)}, u32[]{:S(2)}) copy-start(s32[1,32]{1,0:T(1,128)} %param.46) | copy-start | bytes 388
  38.6 21.4 %all-to-all-start.1 = ((bf16[128,32,128]{0,2,1:T(8,128)(2,1)}), bf16[128,32,128]{0,2,1:T(8,128)(2,1)}, u32[]{:S(2)}, u32[]{:S(2)}) async-start(bf16[128,32,128]{0,2,1:T(8,128)(2,1)} %bitcast.154), calls=%async_computation.1 | async-start | bytes 2097152 | tf_op jit(solution)/shard_map/all_to_all | solution.py:72
  60.0 22.2 %all-to-all-start.3 = ((bf16[128,32,128]{2,0,1:T(8,128)(2,1)}), bf16[128,32,128]{2,0,1:T(8,128)(2,1)}, u32[]{:S(2)}, u32[]{:S(2)}) async-start(bf16[128,32,128]{2,0,1:T(8,128)(2,1)} %copy.147), calls=%async_computation.3 | async-start | bytes 2097152 | tf_op jit(solution)/shard_map/all_to_all | solution.py:93
  82.3 22.2 %all-to-all-start.2 = ((bf16[128,32,128]{0,2,1:T(8,128)(2,1)}), bf16[128,32,128]{0,2,1:T(8,128)(2,1)}, u32[]{:S(2)}, u32[]{:S(2)}) async-start(bf16[128,32,128]{0,2,1:T(8,128)(2,1)} %bitcast.153), calls=%async_computation.2 | async-start | bytes 2097152 | tf_op jit(solution)/shard_map/all_to_all | solution.py:73
  89.1 200.8 %all-gather.3.cloned.1.call-start = ((), (), s32[]{:S(2)}) async-start(), calls=%async_computation.8 | async-start | bytes 9437184 | tf_op jit(solution)/shard_map/all_gather | solution.py:133
  120.6 20.5 %copy-start.38 = (bf16[4096,128]{1,0:T(8,128)(2,1)}, bf16[4096,128]{1,0:T(8,128)(2,1)S(1)}, u32[]{:S(2)}) copy-start(bf16[4096,128]{1,0:T(8,128)(2,1)S(1)} %bitcast_multiply_fusion) | copy-start | bytes 3145732
  127.9 15.3 %copy-start.2 = (bf16[512,1024]{0,1:T(8,128)(2,1)}, bf16[512,1024]{0,1:T(8,128)(2,1)S(1)}, u32[]{:S(2)}) copy-start(bf16[512,1024]{0,1:T(8,128)(2,1)S(1)} %multiply_convert_fusion.5) | copy-start | bytes 3145732
  130.8 13.0 %copy-start.4 = (bf16[512,1024]{0,1:T(8,128)(2,1)}, bf16[512,1024]{0,1:T(8,128)(2,1)S(1)}, u32[]{:S(2)}) copy-start(bf16[512,1024]{0,1:T(8,128)(2,1)S(1)} %multiply_convert_fusion.4) | copy-start | bytes 3145732
  133.8 10.5 %copy-start.6 = (bf16[512,1024]{0,1:T(8,128)(2,1)}, bf16[512,1024]{0,1:T(8,128)(2,1)S(1)}, u32[]{:S(2)}) copy-start(bf16[512,1024]{0,1:T(8,128)(2,1)S(1)} %multiply_convert_fusion.3) | copy-start | bytes 3145732
  136.7 8.1 %copy-start.8 = (bf16[512,1024]{0,1:T(8,128)(2,1)}, bf16[512,1024]{0,1:T(8,128)(2,1)S(1)}, u32[]{:S(2)}) copy-start(bf16[512,1024]{0,1:T(8,128)(2,1)S(1)} %multiply_convert_fusion.2) | copy-start | bytes 3145732
  139.9 5.6 copy-start.10
  170.9 249.3 %all-gather.5.cloned.1.call-start = ((), (), s32[]{:S(2)}) async-start(), calls=%async_computation.9 | async-start | bytes 10485760 | tf_op jit(solution)/shard_map/all_gather | solution.py:137
  171.7 434.6 %reduce-scatter.2.cloned.1.call-start = ((), (), s32[]{:S(2)}) async-start(), calls=%async_computation.10 | async-start | bytes 17825792 | tf_op jit(solution)/shard_map/reduce_scatter | solution.py:141
  311.6 4.8 copy-start.9
  311.6 4.8 copy-start.45
  314.0 4.8 copy-start.11
  314.0 4.8 copy-start.43
  323.3 6.6 %copy-start.31 = (f32[512,512]{0,1:T(8,128)S(1)}, f32[512,512]{0,1:T(8,128)}, u32[]{:S(2)}) copy-start(f32[512,512]{0,1:T(8,128)} %copy-done.30) | copy-start | bytes 3145732
  323.4 33.7 %all-to-all-start.4 = ((f32[32,128,128]{2,1,0:T(8,128)}), f32[32,128,128]{2,1,0:T(8,128)S(1)}, u32[]{:S(2)}, u32[]{:S(2)}) async-start(f32[32,128,128]{2,1,0:T(8,128)} %bitcast.48), calls=%async_computation.4 | async-start | bytes 4194304 | tf_op jit(solution)/shard_map/all_to_all | solution.py:106
  357.0 38.8 %all-to-all-start.5 = ((f32[32,128,128]{2,1,0:T(8,128)}), f32[32,128,128]{2,1,0:T(8,128)}, u32[]{:S(2)}, u32[]{:S(2)}) async-start(f32[32,128,128]{2,1,0:T(8,128)} %bitcast.51), calls=%async_computation.5 | async-start | bytes 4194304 | tf_op jit(solution)/shard_map/all_to_all | solution.py:113
  420.3 186.0 %copy-start.1 = (bf16[1024,1024]{1,0:T(8,128)(2,1)S(1)}, bf16[1024,1024]{1,0:T(8,128)(2,1)}, u32[]{:S(2)}) copy-start(bf16[1024,1024]{1,0:T(8,128)(2,1)} %param.44) | copy-start | bytes 6291460
  (103 other events, 164.8 us)
Sparse Core Ops, SparseCore 0:
  171.1 118.8 all-gather.2
  291.6 128.6 all-gather.4
  423.2 182.9 reduce-scatter.1
where the time goes:
time: 620 us; the launch traced here: 613 us
  waiting for transfers between devices  381 us (61%)
  matrix products  79.8 us (13%)
  starting transfers between devices  48 us (8%)
  local copies, waits for them, and re-layouts  47.1 us (8%)
  blocking collectives  22.1 us (4%)
  other arithmetic  20.2 us (3%)
  between operations  15.2 us (2%)
    reduce_scatter x1, waiting for transfers between devices, body(): lax.psum_scatter(lax.dot_general(used, hidden_in, (((0,), (0,)), ((), ())...  171 us
    all_gather x1, waiting for transfers between devices, body(): block_query = lax.all_gather(shard_query, 'row', axis=0, tiled=True)  118 us
    all_to_all x1, waiting for transfers between devices, body(): lax.all_to_all(grad_value.reshape(group_size, token_dev, HD), ('row', 'co...  26.8 us
    all_to_all x1, blocking collectives, body(): lax.all_to_all(arranged, ('row', 'col'), split_axis=0, concat_axis=1, til...  22.1 us
    all_gather x1, waiting for transfers between devices, body(): lax.all_gather(q_weight, 'col', axis=0, tiled=True)  21.5 us
    dot_general x8, matrix products, attend_head(): jnp.einsum('qk,qd->kd', attention_half, grad_rows, preferred_element_type...  17.4 us
    dot_general x8, matrix products, attend_head(): jnp.einsum('qk,qd->kd', grad_scores, query_rows, preferred_element_type=j...  15.5 us
    dot_general x1, matrix products, body(): lax.dot_general(used, hidden_in, (((0,), (0,)), ((), ())), preferred_elem...  15.2 us
  transfers between devices with their start and end apart: 9, of which 9 were waited for; matrix products, arithmetic and copies ran while one was open for 16% of the time, Pallas kernels for 0%

commit v1 on v0

--- a/solution.py
+++ b/solution.py
@@ -130,7 +130,9 @@
     arranged = grad_query.reshape(columns_count, rows_count, token_dev, heads_dev * HD)
     arranged = arranged.transpose(1, 0, 2, 3).reshape(length_total, heads_dev * HD)
     shard_query = lax.all_to_all(arranged, ("row", "col"), split_axis=0, concat_axis=1, tiled=True)
-    block_query = lax.all_gather(shard_query, "row", axis=0, tiled=True)
+    block_query = jnp.concatenate(
+        lax.all_to_all(jnp.stack([shard_query] * lax.axis_size("row")), "row", 0, 0), axis=0
+    )
     used = block_query
     input_grad = jnp.dot(
         used,

time: 620 us -> 531 us (0.86)
  waiting for transfers between devices: 381 us -> 192 us
  blocking collectives: 22.1 us -> 121 us
    all_gather x1 -> x0, waiting for transfers between devices: 118 us -> none  [body(): block_query = lax.all_gather(shard_query, 'row', axis=0, tiled=True)]
    all_to_all x0 -> x1, blocking collectives: none -> 97.4 us  [body(): lax.all_to_all(jnp.stack([shard_query] * lax.axis_size('row')), 'row', 0, 0)]
    reduce_scatter x1, waiting for transfers between devices: 171 us -> 118 us  [body(): lax.psum_scatter(lax.dot_general(used, hidden_in, (((0,), (0,)), ((), ())...]
    all_gather x1, waiting for transfers between devices: 21.5 us -> 0.01 us  [body(): lax.all_gather(q_weight, 'col', axis=0, tiled=True)]
    slice x9, local copies, waits for them, and re-layouts: 14 us -> 7.76 us  [attend_head(): query_rows = query_all[row_begin:row_end]]
    unnamed x240 -> x254, local copies, waits for them, and re-layouts: 14.8 us -> 13.2 us
  transfers between devices with their start and end apart: 9 -> 8, of which waited for: 9 -> 7; matrix products, arithmetic and copies ran while one was open for 16% -> 25% of each run, Pallas kernels for 0% -> 0%
where the time goes in v1:
time: 531 us; the launch traced here: 524 us
  waiting for transfers between devices  192 us (36%)
  blocking collectives  121 us (23%)
  matrix products  78.2 us (15%)
  starting transfers between devices  49.4 us (9%)
  local copies, waits for them, and re-layouts  44.4 us (8%)
  other arithmetic  21.5 us (4%)
  between operations  17.1 us (3%)
    reduce_scatter x1, waiting for transfers between devices, body(): lax.psum_scatter(lax.dot_general(used, hidden_in, (((0,), (0,)), ((), ())...  118 us
    all_to_all x1, blocking collectives, body(): lax.all_to_all(jnp.stack([shard_query] * lax.axis_size('row')), 'row', 0, 0)  97.4 us
    all_to_all x1, waiting for transfers between devices, body(): lax.all_to_all(grad_value.reshape(group_size, token_dev, HD), ('row', 'co...  28 us
    all_to_all x1, blocking collectives, body(): lax.all_to_all(arranged, ('row', 'col'), split_axis=0, concat_axis=1, til...  24 us
    dot_general x8, matrix products, attend_head(): jnp.einsum('qk,qd->kd', attention_half, grad_rows, preferred_element_type...  16.4 us
    dot_general x8, matrix products, attend_head(): jnp.einsum('qk,qd->kd', grad_scores, query_rows, preferred_element_type=j...  15.6 us
    dot_general x1, matrix products, body(): jnp.dot(used, lax.all_gather(q_weight, 'col', axis=0, tiled=True), prefer...  14.8 us
    dot_general x1, matrix products, body(): lax.dot_general(used, hidden_in, (((0,), (0,)), ((), ())), preferred_elem...  14.6 us
  transfers between devices with their start and end apart: 8, of which 7 were waited for; matrix products, arithmetic and copies ran while one was open for 25% of the time, Pallas kernels for 0%

profile of v1, /device:TPU:1, one launch (start us, length us, event | category | flops | bytes accessed | tf_op | source)
XLA Modules:
  0.0 524.3 jit_solution(7791121332718608042)
XLA Ops:
  11.7 11.3 %all-to-all-start = ((bf16[128,32,128]{2,0,1:T(8,128)(2,1)}), bf16[128,32,128]{2,0,1:T(8,128)(2,1)S(1)}, u32[]{:S(2)}, u32[]{:S(2)}) async-start(bf16[128,32,128]{2,0,1:T(8,128)(2,1)} %copy.144), calls=%async_computation | async-start | bytes 2097152 | tf_op jit(solution)/shard_map/all_to_all | solution.py:92
  26.2 13.2 %all-to-all-done = bf16[128,32,128]{2,0,1:T(8,128)(2,1)S(1)} async-done(((bf16[128,32,128]{2,0,1:T(8,128)(2,1)}), bf16[128,32,128]{2,0,1:T(8,128)(2,1)S(1)}, u32[]{:S(2)}, u32[]{:S(2)}) %all-to-all-start) | async-done | bytes 1048608 | tf_op jit(solution)/shard_map/all_to_all | solution.py:92
  39.3 6.0 %all-to-all-start.1 = ((bf16[128,32,128]{0,2,1:T(8,128)(2,1)}), bf16[128,32,128]{0,2,1:T(8,128)(2,1)}, u32[]{:S(2)}, u32[]{:S(2)}) async-start(bf16[128,32,128]{0,2,1:T(8,128)(2,1)} %bitcast.157), calls=%async_computation.1 | async-start | bytes 2097152 | tf_op jit(solution)/shard_map/all_to_all | solution.py:72
  47.1 2.6 copy.150
  57.3 3.5 all-to-all-done.1
  60.7 8.6 %all-to-all-start.3 = ((bf16[128,32,128]{2,0,1:T(8,128)(2,1)}), bf16[128,32,128]{2,0,1:T(8,128)(2,1)}, u32[]{:S(2)}, u32[]{:S(2)}) async-start(bf16[128,32,128]{2,0,1:T(8,128)(2,1)} %copy.150), calls=%async_computation.3 | async-start | bytes 2097152 | tf_op jit(solution)/shard_map/all_to_all | solution.py:93
  72.6 12.9 %all-to-all-done.3 = bf16[128,32,128]{2,0,1:T(8,128)(2,1)} async-done(((bf16[128,32,128]{2,0,1:T(8,128)(2,1)}), bf16[128,32,128]{2,0,1:T(8,128)(2,1)}, u32[]{:S(2)}, u32[]{:S(2)}) %all-to-all-start.3) | async-done | bytes 1048608 | tf_op jit(solution)/shard_map/all_to_all | solution.py:93
  85.5 8.1 %all-to-all-start.2 = ((bf16[128,32,128]{0,2,1:T(8,128)(2,1)}), bf16[128,32,128]{0,2,1:T(8,128)(2,1)}, u32[]{:S(2)}, u32[]{:S(2)}) async-start(bf16[128,32,128]{0,2,1:T(8,128)(2,1)} %bitcast.156), calls=%async_computation.2 | async-start | bytes 2097152 | tf_op jit(solution)/shard_map/all_to_all | solution.py:73
  100.1 2.8 fusion.102
  102.9 7.0 %all-to-all-done.2 = bf16[128,32,128]{0,2,1:T(8,128)(2,1)} async-done(((bf16[128,32,128]{0,2,1:T(8,128)(2,1)}), bf16[128,32,128]{0,2,1:T(8,128)(2,1)}, u32[]{:S(2)}, u32[]{:S(2)}) %all-to-all-start.2) | async-done | bytes 1048608 | tf_op jit(solution)/shard_map/all_to_all | solution.py:73
  146.5 24.0 %all_to_all.96 = bf16[32,128,128]{2,1,0:T(8,128)(2,1)} all-to-all(bf16[32,128,128]{2,1,0:T(8,128)(2,1)S(1)} %bitcast.158), channel_id=1, replica_groups=mesh['rollout'=4,'row'=8,'col'=4] {'row','col'}, dimensions={0} | all-to-all | bytes 2097152 | tf_op jit(solution)/shard_map/all_to_all | solution.py:132
  177.3 97.4 %all_to_all.97 = bf16[8,128,4096]{2,1,0:T(8,128)(2,1)} all-to-all(bf16[8,128,4096]{2,1,0:T(8,128)(2,1)S(1)} %stack.5), channel_id=1, replica_groups=mesh['rollout'=4,'row'=8,'col'=4] {'row'}, dimensions={0} | all-to-all | bytes 16777216 | tf_op jit(solution)/shard_map/all_to_all | solution.py:134
  274.8 14.6 %fusion.114 = f32[4096,1024]{1,0:T(8,128)} fusion(bf16[1024,4096]{1,0:T(8,128)(2,1)} %bitcast.154, bf16[1024,1024]{1,0:T(8,128)(2,1)S(1)} %copy-done), kind=kOutput, calls=%fused_computation.197 | convolution fusion | flops 8589934592 | bytes 27262976 | tf_op jit(solution)/shard_map/dot_general | solution.py:144
  307.6 5.6 %all-to-all-start.4 = ((f32[32,128,128]{2,1,0:T(8,128)}), f32[32,128,128]{2,1,0:T(8,128)}, u32[]{:S(2)}, u32[]{:S(2)}) async-start(f32[32,128,128]{2,1,0:T(8,128)} %bitcast.48), calls=%async_computation.4 | async-start | bytes 4194304 | tf_op jit(solution)/shard_map/all_to_all | solution.py:106
  317.7 2.5 fusion.23
  320.2 2.5 fusion.22
  322.8 2.5 fusion.21
  325.3 2.5 fusion.20
  327.9 2.5 fusion.19
  332.7 8.9 %all-to-all-done.4 = f32[32,128,128]{2,1,0:T(8,128)} async-done(((f32[32,128,128]{2,1,0:T(8,128)}), f32[32,128,128]{2,1,0:T(8,128)}, u32[]{:S(2)}, u32[]{:S(2)}) %all-to-all-start.4) | async-done | bytes 2097184 | tf_op jit(solution)/shard_map/all_to_all | solution.py:106
  341.5 9.7 %all-to-all-start.5 = ((f32[32,128,128]{2,1,0:T(8,128)}), f32[32,128,128]{2,1,0:T(8,128)S(1)}, u32[]{:S(2)}, u32[]{:S(2)}) async-start(f32[32,128,128]{2,1,0:T(8,128)} %bitcast.51), calls=%async_computation.5 | async-start | bytes 4194304 | tf_op jit(solution)/shard_map/all_to_all | solution.py:113
  354.2 28.0 %all-to-all-done.5 = f32[32,128,128]{2,1,0:T(8,128)S(1)} async-done(((f32[32,128,128]{2,1,0:T(8,128)}), f32[32,128,128]{2,1,0:T(8,128)S(1)}, u32[]{:S(2)}, u32[]{:S(2)}) %all-to-all-start.5) | async-done | bytes 2097184 | tf_op jit(solution)/shard_map/all_to_all | solution.py:113
  383.5 14.8 %convolution_convert_fusion = bf16[1024,1024]{1,0:T(8,128)(2,1)} fusion(bf16[1024,4096]{1,0:T(8,128)(2,1)} %bitcast.155, bf16[4096,1024]{1,0:T(8,128)(2,1)} %all-gather.2.cloned.1.call-done), kind=kOutput, calls=%fused_computation.30 | convolution fusion | flops 8590983168 | bytes 18874368 | tf_op jit(solution)/shard_map/dot_general | solution.py:137
  398.3 118.3 %reduce-scatter.2.cloned.1.call-done = f32[256,1024]{1,0:T(8,128)} async-done(((f32[4096,1024]{1,0:T(8,128)}), f32[256,1024]{1,0:T(8,128)}) %reduce-scatter.2.cloned.1.call-update) | async-done | bytes 1048592 | tf_op jit(solution)/shard_map/reduce_scatter | solution.py:143
  (361 shorter events, 97.6 us)
Async XLA Ops:
  8.0 266.8 %copy-start = (bf16[1024,1024]{1,0:T(8,128)(2,1)S(1)}, bf16[1024,1024]{1,0:T(8,128)(2,1)}, u32[]{:S(2)}) copy-start(bf16[1024,1024]{1,0:T(8,128)(2,1)} %param.44) | copy-start | bytes 6291460
  11.7 27.6 %all-to-all-start = ((bf16[128,32,128]{2,0,1:T(8,128)(2,1)}), bf16[128,32,128]{2,0,1:T(8,128)(2,1)S(1)}, u32[]{:S(2)}, u32[]{:S(2)}) async-start(bf16[128,32,128]{2,0,1:T(8,128)(2,1)} %copy.144), calls=%async_computation | async-start | bytes 2097152 | tf_op jit(solution)/shard_map/all_to_all | solution.py:92
  23.1 360.4 %all-gather.2.cloned.1.call-start = ((), (), s32[]{:S(2)}) async-start(), calls=%async_computation.9 | async-start | bytes 10485760 | tf_op jit(solution)/shard_map/all_gather | solution.py:139
  26.1 20.7 %copy-start.124 = (s32[1,32]{1,0:T(1,128)S(1)}, s32[1,32]{1,0:T(1,128)}, u32[]{:S(2)}) copy-start(s32[1,32]{1,0:T(1,128)} %param.46) | copy-start | bytes 388
  39.3 21.4 %all-to-all-start.1 = ((bf16[128,32,128]{0,2,1:T(8,128)(2,1)}), bf16[128,32,128]{0,2,1:T(8,128)(2,1)}, u32[]{:S(2)}, u32[]{:S(2)}) async-start(bf16[128,32,128]{0,2,1:T(8,128)(2,1)} %bitcast.157), calls=%async_computation.1 | async-start | bytes 2097152 | tf_op jit(solution)/shard_map/all_to_all | solution.py:72
  60.7 24.7 %all-to-all-start.3 = ((bf16[128,32,128]{2,0,1:T(8,128)(2,1)}), bf16[128,32,128]{2,0,1:T(8,128)(2,1)}, u32[]{:S(2)}, u32[]{:S(2)}) async-start(bf16[128,32,128]{2,0,1:T(8,128)(2,1)} %copy.150), calls=%async_computation.3 | async-start | bytes 2097152 | tf_op jit(solution)/shard_map/all_to_all | solution.py:93
  85.5 24.4 %all-to-all-start.2 = ((bf16[128,32,128]{0,2,1:T(8,128)(2,1)}), bf16[128,32,128]{0,2,1:T(8,128)(2,1)}, u32[]{:S(2)}, u32[]{:S(2)}) async-start(bf16[128,32,128]{0,2,1:T(8,128)(2,1)} %bitcast.156), calls=%async_computation.2 | async-start | bytes 2097152 | tf_op jit(solution)/shard_map/all_to_all | solution.py:73
  93.5 423.1 %reduce-scatter.2.cloned.1.call-start = ((), (), s32[]{:S(2)}) async-start(), calls=%async_computation.10 | async-start | bytes 17825792 | tf_op jit(solution)/shard_map/reduce_scatter | solution.py:143
  100.1 12.1 %copy-start.58 = (bf16[4,128,128]{1,2,0:T(8,128)(2,1)S(1)}, bf16[4,128,128]{1,2,0:T(8,128)(2,1)}, u32[]{:S(2)}) copy-start(bf16[4,128,128]{1,2,0:T(8,128)(2,1)} %get-tuple-element.202) | copy-start | bytes 393220
  102.9 10.0 %copy-start.57 = (bf16[4,128,128]{1,2,0:T(8,128)(2,1)S(1)}, bf16[4,128,128]{1,2,0:T(8,128)(2,1)}, u32[]{:S(2)}) copy-start(bf16[4,128,128]{1,2,0:T(8,128)(2,1)} %get-tuple-element.201) | copy-start | bytes 393220
  102.9 10.8 %copy-start.56 = (bf16[4,128,128]{1,2,0:T(8,128)(2,1)S(1)}, bf16[4,128,128]{1,2,0:T(8,128)(2,1)}, u32[]{:S(2)}) copy-start(bf16[4,128,128]{1,2,0:T(8,128)(2,1)} %get-tuple-element.200) | copy-start | bytes 393220
  102.9 11.6 %copy-start.55 = (bf16[4,128,128]{1,2,0:T(8,128)(2,1)S(1)}, bf16[4,128,128]{1,2,0:T(8,128)(2,1)}, u32[]{:S(2)}) copy-start(bf16[4,128,128]{1,2,0:T(8,128)(2,1)} %get-tuple-element.199) | copy-start | bytes 393220
  102.9 12.3 %copy-start.54 = (bf16[4,128,128]{1,2,0:T(8,128)(2,1)S(1)}, bf16[4,128,128]{1,2,0:T(8,128)(2,1)}, u32[]{:S(2)}) copy-start(bf16[4,128,128]{1,2,0:T(8,128)(2,1)} %get-tuple-element.198) | copy-start | bytes 393220
  102.9 13.1 %copy-start.53 = (bf16[4,128,128]{1,2,0:T(8,128)(2,1)S(1)}, bf16[4,128,128]{1,2,0:T(8,128)(2,1)}, u32[]{:S(2)}) copy-start(bf16[4,128,128]{1,2,0:T(8,128)(2,1)} %get-tuple-element.197) | copy-start | bytes 393220
  102.9 13.9 %copy-start.52 = (bf16[4,128,128]{1,2,0:T(8,128)(2,1)S(1)}, bf16[4,128,128]{1,2,0:T(8,128)(2,1)}, u32[]{:S(2)}) copy-start(bf16[4,128,128]{1,2,0:T(8,128)(2,1)} %get-tuple-element.196) | copy-start | bytes 393220
  121.5 23.2 %copy-start.38 = (bf16[4096,128]{1,0:T(8,128)(2,1)}, bf16[4096,128]{1,0:T(8,128)(2,1)S(1)}, u32[]{:S(2)}) copy-start(bf16[4096,128]{1,0:T(8,128)(2,1)S(1)} %bitcast_multiply_fusion) | copy-start | bytes 3145732
  128.8 12.0 %copy-start.2 = (bf16[512,1024]{0,1:T(8,128)(2,1)}, bf16[512,1024]{0,1:T(8,128)(2,1)S(1)}, u32[]{:S(2)}) copy-start(bf16[512,1024]{0,1:T(8,128)(2,1)S(1)} %multiply_convert_fusion.5) | copy-start | bytes 3145732
  131.7 9.6 %copy-start.4 = (bf16[512,1024]{0,1:T(8,128)(2,1)}, bf16[512,1024]{0,1:T(8,128)(2,1)S(1)}, u32[]{:S(2)}) copy-start(bf16[512,1024]{0,1:T(8,128)(2,1)S(1)} %multiply_convert_fusion.4) | copy-start | bytes 3145732
  134.7 7.2 %copy-start.6 = (bf16[512,1024]{0,1:T(8,128)(2,1)}, bf16[512,1024]{0,1:T(8,128)(2,1)S(1)}, u32[]{:S(2)}) copy-start(bf16[512,1024]{0,1:T(8,128)(2,1)S(1)} %multiply_convert_fusion.3) | copy-start | bytes 3145732
  145.9 24.6 %copy-start.12 = (bf16[512,1024]{0,1:T(8,128)(2,1)}, bf16[512,1024]{0,1:T(8,128)(2,1)S(1)}, u32[]{:S(2)}) copy-start(bf16[512,1024]{0,1:T(8,128)(2,1)S(1)} %multiply_convert_fusion) | copy-start | bytes 3145732
  307.6 5.6 %copy-start.39 = (bf16[4096,128]{1,0:T(8,128)(2,1)S(1)}, bf16[4096,128]{1,0:T(8,128)(2,1)}, u32[]{:S(2)}) copy-start(bf16[4096,128]{1,0:T(8,128)(2,1)} %copy-done.38) | copy-start | bytes 3145732
  307.6 34.0 %all-to-all-start.4 = ((f32[32,128,128]{2,1,0:T(8,128)}), f32[32,128,128]{2,1,0:T(8,128)}, u32[]{:S(2)}, u32[]{:S(2)}) async-start(f32[32,128,128]{2,1,0:T(8,128)} %bitcast.48), calls=%async_computation.4 | async-start | bytes 4194304 | tf_op jit(solution)/shard_map/all_to_all | solution.py:106
  341.5 40.6 %all-to-all-start.5 = ((f32[32,128,128]{2,1,0:T(8,128)}), f32[32,128,128]{2,1,0:T(8,128)S(1)}, u32[]{:S(2)}, u32[]{:S(2)}) async-start(f32[32,128,128]{2,1,0:T(8,128)} %bitcast.51), calls=%async_computation.5 | async-start | bytes 4194304 | tf_op jit(solution)/shard_map/all_to_all | solution.py:113
  383.5 133.1 %copy-start.1 = (bf16[1024,1024]{1,0:T(8,128)(2,1)S(1)}, bf16[1024,1024]{1,0:T(8,128)(2,1)}, u32[]{:S(2)}) copy-start(bf16[1024,1024]{1,0:T(8,128)(2,1)} %param.44) | copy-start | bytes 6291460
  (109 other events, 220.3 us)
Sparse Core Ops, SparseCore 0:
  25.6 118.6 all-gather.1
Sparse Core Ops, SparseCore 1:
  289.5 227.0 reduce-scatter.1
